TPU v7x, 32 devices: a whole 2x2x4 slice. The times are simulated.
32 devices in a mesh: row: 4 (over x, core), col: 8 (over z, y).
Axes of the slice: x: 2, y: 2, z: 4, core: 2. Of those that a mesh axis runs over, the one named last changes fastest.
Arguments:
- iterate: bfloat16 [4096, 8192], P('row', 'col'), may hold values from -0.5 to 0.5, as said below
Outputs:
- update: float32 [4096, 8192], P('row', 'col')
Inputs may be any that keep to these rules, and one draw needn't show every extreme that they name: One iterate of the orthogonalization.
All inputs are finite; a program needn't handle non-finite values.
Results may differ from a plain program's by a relative error of at most 0.0041.
Values may be sent and summed in bfloat16 or wider, within the bound.
A program may use at most 64 MiB of HBM per device.

v0:
```python
import math

import jax
import jax.numpy as jnp
from jax import lax
from jax.sharding import PartitionSpec as P

COLS = 8192


coef_a = 3.4445
coef_b = -4.775
coef_c = 2.0315


def per_device(iterate):
    cols_x = lax.all_gather(iterate, "row", axis=0, tiled=True)
    mirrored = lax.psum_scatter(
        lax.dot_general(
            cols_x, iterate, (((1,), (1,)), ((), ())), preferred_element_type=jnp.float32
        ),
        "col",
        scatter_dimension=0,
        tiled=True,
    )
    gram_block = mirrored.T.astype(jnp.bfloat16)
    gram_cols = lax.all_gather(gram_block, "row", axis=0, tiled=True)
    lower = gram_cols
    square = jnp.dot(
        lax.all_gather(gram_block, "col", axis=1, tiled=True),
        lower,
        preferred_element_type=jnp.float32,
    )
    poly = (coef_b * gram_block.astype(jnp.float32) + coef_c * square).astype(jnp.bfloat16)
    lower = cols_x
    mixed = jnp.dot(
        lax.all_gather(poly, "col", axis=1, tiled=True), lower, preferred_element_type=jnp.float32
    )
    return math.sqrt(COLS) * (coef_a * iterate.astype(jnp.float32) + mixed)


def solution(mesh):
    placed = (P("row", "col"),)
    return jax.shard_map(
        per_device, mesh=mesh, in_specs=placed, out_specs=P("row", "col"), check_vma=False
    )
```

profile of v0, /device:TPU:0, one launch (start us, length us, event | category | flops | bytes accessed | tf_op | source)
XLA Modules:
  0.0 684.1 jit_solution(4347285785540661950)
XLA Ops:
  6.5 0.0 all-gather.5.cloned.1.call-start
  6.5 0.7 all-gather.5.cloned.1.call-update
  7.3 0.0 reduce-scatter.2.cloned.1.call-start
  7.3 62.6 %all-gather.5.cloned.1.call-done = bf16[4096,1024]{1,0:T(8,128)(2,1)} async-done(((bf16[1024,1024]{1,0:T(8,128)(2,1)}), bf16[4096,1024]{1,0:T(8,128)(2,1)}) %all-gather.5.cloned.1.call-update) | async-done | bytes 8388624 | tf_op jit(solution)/shard_map/all_gather | solution.py:17
  69.9 16.1 %fusion = f32[4096,1024]{1,0:T(8,128)} fusion(bf16[4096,1024]{1,0:T(8,128)(2,1)} %all-gather.5.cloned.1.call-done, bf16[1024,1024]{1,0:T(8,128)(2,1)} %param.1), kind=kOutput, calls=%fused_computation.3 | convolution fusion | flops 8589934592 | bytes 27262976 | tf_op jit(solution)/shard_map/dot_general | solution.py:19
  86.1 0.0 reduce-scatter.2.cloned.1.call-update
  86.1 0.0 all-gather.9.cloned.1.call-start
  86.1 280.3 %reduce-scatter.2.cloned.1.call-done = f32[512,1024]{1,0:T(8,128)} async-done(((f32[4096,1024]{1,0:T(8,128)}), f32[512,1024]{1,0:T(8,128)}) %reduce-scatter.2.cloned.1.call-update) | async-done | bytes 2097168 | tf_op jit(solution)/shard_map/reduce_scatter | solution.py:18
  366.5 2.7 convert_bitcast_fusion
  369.2 0.0 all-gather.9.cloned.1.call-update
  369.2 0.0 all-gather.7.cloned.1.call-start
  369.2 0.5 all-gather.7.cloned.1.call-update
  369.8 0.0 copy-start
  369.8 0.0 all-gather.11.cloned.1.call-start
  369.8 33.1 %all-gather.9.cloned.1.call-done = bf16[4096,512]{0,1:T(8,128)(2,1)} async-done(((bf16[1024,512]{0,1:T(8,128)(2,1)}), bf16[4096,512]{0,1:T(8,128)(2,1)}) %all-gather.9.cloned.1.call-update) | async-done | bytes 4194320 | tf_op jit(solution)/shard_map/all_gather | solution.py:27
  402.9 126.5 %all-gather.7.cloned.1.call-done = bf16[1024,4096]{0,1:T(8,128)(2,1)} async-done(((bf16[1024,512]{0,1:T(8,128)(2,1)}), bf16[1024,4096]{0,1:T(8,128)(2,1)}) %all-gather.7.cloned.1.call-update) | async-done | bytes 8388624 | tf_op jit(solution)/shard_map/all_gather | solution.py:30
  529.4 10.3 %add_convert_fusion = bf16[1024,512]{0,1:T(8,128)(2,1)} fusion(bf16[1024,512]{0,1:T(8,128)(2,1)} %convert_bitcast_fusion, bf16[4096,512]{0,1:T(8,128)(2,1)} %all-gather.9.cloned.1.call-done, bf16[1024,4096]{0,1:T(8,128)(2,1)} %all-gather.7.cloned.1.call-done), kind=kOutput, calls=%fused_computation.1 | convolution fusion | flops 4297588736 | bytes 14680064 | tf_op jit(solution)/shard_map/dot_general | solution.py:29
  539.7 0.0 all-gather.11.cloned.1.call-update
  539.7 122.8 %all-gather.11.cloned.1.call-done = bf16[1024,4096]{0,1:T(8,128)(2,1)} async-done(((bf16[1024,512]{0,1:T(8,128)(2,1)}), bf16[1024,4096]{0,1:T(8,128)(2,1)}) %all-gather.11.cloned.1.call-update) | async-done | bytes 8388624 | tf_op jit(solution)/shard_map/all_gather | solution.py:37
  662.5 0.0 copy-done
  662.5 15.1 %add_multiply_fusion = f32[1024,1024]{1,0:T(8,128)} fusion(bf16[1024,1024]{1,0:T(8,128)(2,1)S(1)} %copy-done, bf16[1024,4096]{0,1:T(8,128)(2,1)} %all-gather.11.cloned.1.call-done, bf16[4096,1024]{1,0:T(8,128)(2,1)} %all-gather.5.cloned.1.call-done), kind=kOutput, calls=%fused_computation | convolution fusion | flops 8594128896 | bytes 23068672 | tf_op jit(solution)/shard_map/dot_general | solution.py:36
Async XLA Ops:
  6.5 63.4 %all-gather.5.cloned.1.call-start = ((), (), s32[]{:S(2)}) async-start(), calls=%async_computation.1 | async-start | bytes 10485760 | tf_op jit(solution)/shard_map/all_gather | solution.py:17
  7.3 359.2 %reduce-scatter.2.cloned.1.call-start = ((), (), s32[]{:S(2)}) async-start(), calls=%async_computation.2 | async-start | bytes 18874368 | tf_op jit(solution)/shard_map/reduce_scatter | solution.py:18
  86.1 316.8 %all-gather.9.cloned.1.call-start = ((), (), s32[]{:S(2)}) async-start(), calls=%async_computation.4 | async-start | bytes 5242880 | tf_op jit(solution)/shard_map/all_gather | solution.py:27
  369.2 160.2 %all-gather.7.cloned.1.call-start = ((), (), s32[]{:S(2)}) async-start(), calls=%async_computation.3 | async-start | bytes 9437184 | tf_op jit(solution)/shard_map/all_gather | solution.py:30
  369.8 292.8 %copy-start = (bf16[1024,1024]{1,0:T(8,128)(2,1)S(1)}, bf16[1024,1024]{1,0:T(8,128)(2,1)}, u32[]{:S(2)}) copy-start(bf16[1024,1024]{1,0:T(8,128)(2,1)} %param.1) | copy-start | bytes 6291460
  369.8 292.7 %all-gather.11.cloned.1.call-start = ((), (), s32[]{:S(2)}) async-start(), calls=%async_computation.5 | async-start | bytes 9437184 | tf_op jit(solution)/shard_map/all_gather | solution.py:37
Sparse Core Ops, SparseCore 0:
  8.9 60.9 all-gather.4
  86.2 280.2 reduce-scatter.1
  369.3 33.5 all-gather.8
  404.9 124.4 all-gather.6
  539.8 122.6 all-gather.10
where the time goes:
time: 684 us
  waiting for transfers between devices  627 us (92%)
  matrix products  41.5 us (6%)
  between operations  13.1 us (2%)
    reduce_scatter x1, waiting for transfers between devices, per_device(): lax.psum_scatter(lax.dot_general(cols_x, iterate, (((1,), (1,)), ((), ())...  280 us
    all_gather x1, waiting for transfers between devices, per_device(): lax.all_gather(gram_block, 'col', axis=1, tiled=True)  126 us
    all_gather x1, waiting for transfers between devices, per_device(): lax.all_gather(poly, 'col', axis=1, tiled=True)  123 us
    all_gather x1, waiting for transfers between devices, per_device(): cols_x = lax.all_gather(iterate, 'row', axis=0, tiled=True)  62.6 us
    all_gather x1, waiting for transfers between devices, per_device(): gram_cols = lax.all_gather(gram_block, 'row', axis=0, tiled=True)  33.1 us
    dot_general x1, matrix products, per_device(): lax.dot_general(cols_x, iterate, (((1,), (1,)), ((), ())), preferred_elem...  16.1 us
    dot_general x1, matrix products, per_device(): jnp.dot(lax.all_gather(poly, 'col', axis=1, tiled=True), lower, preferred...  15.1 us
  transfers between devices with their start and end apart: 5, of which 5 were waited for; matrix products, arithmetic and copies ran while one was open for 0% of the time, Pallas kernels for 0%

commit v1 on v0

v1 whole, which is shorter than its diff:
```python
import functools
import math

import jax
import jax.numpy as jnp
from jax import lax
from jax.experimental import pallas as pl
from jax.experimental.pallas import tpu as pltpu
from jax.sharding import PartitionSpec as P

MESH = pl.DeviceIdType.MESH
coef_a = 3.4445
coef_b = -4.775
coef_c = 2.0315
SLICES = 2
PIECES = 4


def kernel(
    R, C, scale, x_ref, o_ref, xc, zc, rs, g, y,
    sx, qx, sr, qr, sa, qa, sz, qz,
):
    B, W = x_ref.shape
    T = R // 2
    w = 2 * B // C
    hb = B // 2
    nr = hb // SLICES
    f32, bf16 = jnp.float32, jnp.bfloat16

    r, c = lax.axis_index("row"), lax.axis_index("col")
    odd = lax.rem(c, 2)
    p = (1 - odd) * lax.div(c, 2) + odd * (C - 1 - lax.div(c, 2))

    def col_at(q):
        q = lax.rem(q + C, C)
        hi = lax.div(q, C // 2)
        return (1 - hi) * (2 * q) + hi * (2 * (C - 1 - q) + 1)

    def chunk(q):
        return lax.rem(q + 2 * C, C)

    ring = ((r, col_at(p + 1)), (r, col_at(p - 1)))
    mate = (r + 1 - 2 * lax.rem(r, 2), c)

    def peer(j):
        return (lax.rem(r + 2 * j, R), c)

    def rows_of(row):
        return row * B

    def start_of(t):
        return lax.rem(lax.div(r, 2) + t, T) * (2 * B)

    def hops(u, d):
        return C // 2 if u == d else C - 1 - C // 2

    barrier = pltpu.get_barrier_semaphore()
    friends = [ring[0], ring[1], mate] + [peer(j) for j in range(1, T)]
    for f in friends:
        pl.semaphore_signal(barrier, inc=1, device_id=f, device_id_type=MESH)
    pl.semaphore_wait(barrier, len(friends))

    sent = []

    def send(src, dst, ssem, rsem, to):
        cp = pltpu.make_async_remote_copy(
            src_ref=src, dst_ref=dst, send_sem=ssem, recv_sem=rsem,
            device_id=to, device_id_type=MESH,
        )
        cp.start()
        sent.append(cp)

    def wait_recv(ref, rsem):
        pltpu.make_async_remote_copy(
            src_ref=ref, dst_ref=ref, send_sem=rsem, recv_sem=rsem,
            device_id=mate, device_id_type=MESH,
        ).wait_recv()

    def rows(base, n):
        return pl.ds(pl.multiple_of(base, n), n)

    pr = B // PIECES
    here = rows(r * B, B)
    own = pltpu.make_async_copy(x_ref, xc.at[here, :], sx.at[0, 0])
    own.start()
    send(x_ref, xc.at[here, :], sx.at[0, 1], qx.at[0, 1], mate)
    for i in range(PIECES):
        for j in range(1, T):
            send(
                x_ref.at[pl.ds(i * pr, pr), :],
                xc.at[rows(r * B + i * pr, pr), :],
                sx.at[j, i], qx.at[j, i], peer(j),
            )

    def forward_x(i):
        for j in range(1, T):
            src = lax.rem(r + R - 2 * j, R)
            ref = xc.at[rows(src * B + i * pr, pr), :]
            wait_recv(ref, qx.at[j, i])
            send(ref, ref, sx.at[T + j, i], qx.at[T + j, i], mate)

    def finish_x():
        for i in range(PIECES):
            for j in range(1, T):
                src = lax.rem(mate[0] + R - 2 * j, R)
                wait_recv(xc.at[rows(src * B + i * pr, pr), :], qx.at[T + j, i])

    own.wait()
    wait_recv(xc.at[rows(mate[0] * B, B), :], qx.at[0, 1])

    def part(t, q, u):
        return lax.dot_general(
            x_ref[u * hb : (u + 1) * hb, :],
            xc[rows(start_of(t) + q * w, w), :],
            (((1,), (1,)), ((), ())),
            preferred_element_type=f32,
        )

    for t in range(T):
        for s in range(C // 2 + 1):
            for u in range(2):
                for d in range(2):
                    n = hops(u, d)
                    if s >= n:
                        continue
                    q = chunk(p + (n - s)) if d == 0 else chunk(p - (n - s))
                    v = part(t, q, u)
                    buf = rs.at[t, u, d, s]
                    if s > 0:
                        wait_recv(buf, qr.at[t, u, d, s - 1])
                        v = v + buf[...].astype(f32)
                    buf[...] = v.astype(bf16)
                    send(buf, rs.at[t, u, d, s + 1], sr.at[t, u, d, s], qr.at[t, u, d, s], ring[d])
            if t == 0 and 0 < s <= PIECES:
                forward_x(s - 1)
        if t == 0:
            for i in range(min(C // 2, PIECES), PIECES):
                forward_x(i)
        for u in range(2):
            v = part(t, p, u)
            for d in range(2):
                n = hops(u, d)
                buf = rs.at[t, u, d, n]
                wait_recv(buf, qr.at[t, u, d, n - 1])
                v = v + buf[...].astype(f32)
            g[p, t, u * hb : (u + 1) * hb, :] = v.astype(bf16)
        if t == 0:
            finish_x()

    def add_y(q, u, h, first=False):
        rr = pl.ds(u * hb + h * nr, nr)
        v = None
        for t in range(T):
            m = jnp.dot(
                g[q, t, rr, :], xc[rows(start_of(t) + q * w, w), :], preferred_element_type=f32
            )
            v = m if v is None else v + m
        if first:
            y[rr, :] = v
        else:
            y[rr, :] += v

    def send_g(h, u, d, s):
        q = chunk(p - s) if d == 0 else chunk(p + s)
        ref = g.at[q, :, pl.ds(u * hb + h * nr, nr), :]
        send(ref, ref, sa.at[h, u, d, s], qa.at[h, u, d, s], ring[d])

    def zref(row, u, h):
        return zc.at[rows(row * B + u * hb + h * nr, nr), :]

    def forward_z(h, u):
        for j in range(1, T):
            ref = zref(lax.rem(r + R - 2 * j, R), u, h)
            wait_recv(ref, qz.at[h, u, j])
            send(ref, ref, sz.at[h, u, T + j], qz.at[h, u, T + j], mate)

    def finish_z(h, u):
        for j in range(1, T):
            wait_recv(zref(lax.rem(mate[0] + R - 2 * j, R), u, h), qz.at[h, u, T + j])

    for u in range(2):
        for d in range(2):
            send_g(0, u, d, 0)
    for h in range(SLICES):
        for u in range(2):
            add_y(p, u, h, first=True)
        last = C // 2 - 1
        for s in range(last + 1):
            if s == last and h > 0:
                for u in range(2):
                    forward_z(h - 1, u)
            for u in range(2):
                for d in range(2):
                    n = hops(u, d)
                    if s >= n:
                        continue
                    q = chunk(p - 1 - s) if d == 0 else chunk(p + 1 + s)
                    wait_recv(g.at[q, :, pl.ds(u * hb + h * nr, nr), :], qa.at[h, u, d, s])
                    if s + 1 < n:
                        send_g(h, u, d, s + 1)
                    if s == last - 1 and h + 1 < SLICES:
                        send_g(h + 1, u, d, 0)
                    add_y(q, u, h)
        for u in range(2):
            rr = pl.ds(u * hb + h * nr, nr)
            mine = zref(r, u, h)
            mine[...] = y[rr, :].astype(bf16)
            for j in range(1, T):
                send(mine, mine, sz.at[h, u, j], qz.at[h, u, j], peer(j))
            send(mine, mine, sz.at[h, u, 0], qz.at[h, u, 0], mate)

    tile = min(B, 256)

    def add_out(terms, final=False):
        @pl.loop(0, B // tile)
        def _(i):
            rr = rows(i * tile, tile)
            v = jnp.zeros((tile, W), f32)
            for t, e, u, h in terms:
                k = e * B + u * hb + h * nr
                for k0 in range(k, k + nr, min(w, nr)):
                    n = min(w, nr)
                    q, off = k0 // w, k0 % w
                    v = v + jnp.dot(
                        g[q, t, rr, off : off + n],
                        zc[rows(start_of(t) + k0, n), :],
                        preferred_element_type=f32,
                    )
            if final:
                o_ref[rr, :] = scale * (y[rr, :] + coef_c * v)
            else:
                y[rr, :] += coef_c * v

    @pl.loop(0, B // tile)
    def _(i):
        rr = rows(i * tile, tile)
        y[rr, :] = coef_a * x_ref[rr, :].astype(f32) + coef_b * y[rr, :]

    L = SLICES - 1
    for h in range(SLICES):
        for u in range(2):
            wait_recv(zref(mate[0], u, h), qz.at[h, u, 0])
    for h in range(L):
        for u in range(2):
            finish_z(h, u)
    for h in range(SLICES):
        add_out([(0, e, u, h) for e in range(2) for u in range(2)])
    forward_z(L, 0)
    for h in range(L):
        for t in range(1, T):
            add_out([(t, e, u, h) for e in range(2) for u in range(2)])
    forward_z(L, 1)
    finish_z(L, 0)
    for t in range(1, T):
        add_out([(t, e, 0, L) for e in range(2)])
    finish_z(L, 1)
    for t in range(1, T):
        add_out([(t, e, 1, L) for e in range(2)], final=t == T - 1)

    for cp in sent:
        cp.wait_send()


def solution(mesh):
    R, C = mesh.shape["row"], mesh.shape["col"]

    def step(x):
        B, W = x.shape
        T = R // 2
        w = 2 * B // C
        dma = pltpu.SemaphoreType.DMA
        bf16 = jnp.bfloat16
        rs_sems = (T, 2, 2, C // 2)
        ag_sems = (SLICES, 2, 2, C // 2)
        return pl.pallas_call(
            functools.partial(kernel, R, C, math.sqrt(W * C)),
            out_shape=jax.ShapeDtypeStruct((B, W), jnp.float32),
            in_specs=[pl.BlockSpec(memory_space=pltpu.VMEM)],
            out_specs=pl.BlockSpec(memory_space=pltpu.VMEM),
            scratch_shapes=[
                pltpu.VMEM((R * B, W), bf16),
                pltpu.VMEM((R * B, W), bf16),
                pltpu.VMEM((T, 2, 2, C // 2 + 1, B // 2, w), bf16),
                pltpu.VMEM((C, T, B, w), bf16),
                pltpu.VMEM((B, W), jnp.float32),
                dma((2 * T, PIECES)), dma((2 * T, PIECES)),
                dma(rs_sems), dma(rs_sems),
                dma(ag_sems), dma(ag_sems),
                dma((SLICES, 2, 2 * T)), dma((SLICES, 2, 2 * T)),
            ],
            compiler_params=pltpu.CompilerParams(
                collective_id=0, has_side_effects=True, vmem_limit_bytes=67043328
            ),
        )(x)

    return jax.shard_map(
        step, mesh=mesh, in_specs=(P("row", "col"),), out_specs=P("row", "col"), check_vma=False
    )
```

time: 684 us -> 215 us (0.31)
  waiting for transfers between devices: 627 us -> 0 us
  Pallas kernels: 0 us -> 210 us
  matrix products: 41.5 us -> 0 us
  between operations: 13.1 us -> 0.01 us
    all_gather x4 -> x0, waiting for transfers between devices: 345 us -> none  [the longest x1 126 us: per_device(): lax.all_gather(gram_block, 'col', axis=1, tiled=True)]
    reduce_scatter x1 -> x0, waiting for transfers between devices: 280 us -> none  [per_device(): lax.psum_scatter(lax.dot_general(cols_x, iterate, (((1,), (1,)), ((), ())...]
    pallas_call x0 -> x1, Pallas kernels: none -> 210 us  [step(): pl.pallas_call(functools.partial(kernel, R, C, math.sqrt(W * C)), out_sha...]
    dot_general x3 -> x0, matrix products: 41.5 us -> none  [the longest x1 16.1 us: per_device(): lax.dot_general(cols_x, iterate, (((1,), (1,)), ((), ())), preferred_elem...]
  transfers between devices with their start and end apart: 5 -> 0, of which waited for: 5 -> 0; matrix products, arithmetic and copies ran while one was open for 0% -> 0% of each run, Pallas kernels for 0% -> 0%
where the time goes in v1:
time: 215 us; the launch traced here: 214 us
  Pallas kernels  210 us (98%)
  local copies, waits for them, and re-layouts  4.79 us (2%)
    pallas_call x1, Pallas kernels, step(): pl.pallas_call(functools.partial(kernel, R, C, math.sqrt(W * C)), out_sha...  210 us
    unnamed x1, local copies, waits for them, and re-layouts  4.79 us

profile of v1, /device:TPU:0, one launch (start us, length us, event | category | flops | bytes accessed | tf_op | source)
XLA Modules:
  0.0 214.3 jit_solution(8398565603411557690)
XLA Ops:
  0.0 209.5 %shard_map.17 = f32[1024,1024]{1,0:T(8,128)} custom-call(bf16[1024,1024]{1,0:T(8,128)(2,1)} %x_ref.1), custom_call_target="tpu_custom_call" | custom-call | tf_op jit(solution)/shard_map/pallas_call | solution.py:275
  209.6 4.8 %copy.3 = f32[1024,1024]{1,0:T(8,128)} copy(f32[1024,1024]{1,0:T(8,128)} %shard_map.17) | data formatting | bytes 8388608

commit v2 on v1

--- a/solution.py
+++ b/solution.py
@@ -12,8 +12,14 @@
 coef_a = 3.4445
 coef_b = -4.775
 coef_c = 2.0315
-SLICES = 2
+SLICES = 4
 PIECES = 4
+
+
+def split(B, C):
+    w = 2 * B // C
+    f = 2 if w % 256 == 0 else 1
+    return f, w // f
 
 
 def kernel(
@@ -22,9 +28,10 @@
 ):
     B, W = x_ref.shape
     T = R // 2
-    w = 2 * B // C
+    HF, ww = split(B, C)
     hb = B // 2
     nr = hb // SLICES
+    half = C // 2
     f32, bf16 = jnp.float32, jnp.bfloat16
 
     r, c = lax.axis_index("row"), lax.axis_index("col")
@@ -99,62 +106,92 @@
             wait_recv(ref, qx.at[j, i])
             send(ref, ref, sx.at[T + j, i], qx.at[T + j, i], mate)
 
-    def finish_x():
-        for i in range(PIECES):
-            for j in range(1, T):
-                src = lax.rem(mate[0] + R - 2 * j, R)
-                wait_recv(xc.at[rows(src * B + i * pr, pr), :], qx.at[T + j, i])
+    def finish_x(i):
+        for j in range(1, T):
+            src = lax.rem(mate[0] + R - 2 * j, R)
+            wait_recv(xc.at[rows(src * B + i * pr, pr), :], qx.at[T + j, i])
 
     own.wait()
     wait_recv(xc.at[rows(mate[0] * B, B), :], qx.at[0, 1])
 
-    def part(t, q, u):
-        return lax.dot_general(
-            x_ref[u * hb : (u + 1) * hb, :],
-            xc[rows(start_of(t) + q * w, w), :],
-            (((1,), (1,)), ((), ())),
-            preferred_element_type=f32,
-        )
-
-    for t in range(T):
-        for s in range(C // 2 + 1):
+    def at(t, f, q):
+        e, o = lax.div(q, half), lax.rem(q, half)
+        return rows(start_of(t) + e * B + f * (B // HF) + o * ww, ww)
+
+    phases = [(0, f) for f in range(HF)] + [(t, f) for f in range(HF) for t in range(1, T)]
+    per = PIECES // HF
+    if HF == 2:
+        pass_on = {(0, 2): 0, (1, 0): 1, (1, half - 1): 2, (2, 1): 3}
+    else:
+        pass_on = {(0, i): i for i in range(PIECES)}
+    ready = {HF + f * (T - 1): range(f * per, (f + 1) * per) for f in range(HF)}
+
+    side = min(hb, 256)
+
+    def add_part(k, q, u, came, dst):
+        t, f = phases[k]
+
+        @pl.loop(0, hb // side)
+        def _(i):
+            v = lax.dot_general(
+                x_ref[rows(u * hb + i * side, side), :],
+                xc[at(t, f, q), :],
+                (((1,), (1,)), ((), ())),
+                preferred_element_type=f32,
+            )
+            for ref in came:
+                v = v + ref[rows(i * side, side), :].astype(f32)
+            dst[rows(i * side, side), :] = v.astype(bf16)
+
+    def send_part(k, u, d, s):
+        buf = rs.at[k, u, d, s]
+        add_part(k, toward(u, d, s), u, [buf] if s else [], buf)
+        send(buf, rs.at[k, u, d, s + 1], sr.at[k, u, d, s], qr.at[k, u, d, s], ring[d])
+
+    def toward(u, d, s):
+        n = hops(u, d)
+        return chunk(p + (n - s)) if d == 0 else chunk(p - (n - s))
+
+    def begin(k):
+        for i in ready.get(k, ()):
+            finish_x(i)
+        for u in range(2):
+            for d in range(2):
+                send_part(k, u, d, 0)
+
+    begin(0)
+    for k, (t, f) in enumerate(phases):
+        if (k, 0) in pass_on:
+            forward_x(pass_on[k, 0])
+        for s in range(1, half):
             for u in range(2):
                 for d in range(2):
-                    n = hops(u, d)
-                    if s >= n:
-                        continue
-                    q = chunk(p + (n - s)) if d == 0 else chunk(p - (n - s))
-                    v = part(t, q, u)
-                    buf = rs.at[t, u, d, s]
-                    if s > 0:
-                        wait_recv(buf, qr.at[t, u, d, s - 1])
-                        v = v + buf[...].astype(f32)
-                    buf[...] = v.astype(bf16)
-                    send(buf, rs.at[t, u, d, s + 1], sr.at[t, u, d, s], qr.at[t, u, d, s], ring[d])
-            if t == 0 and 0 < s <= PIECES:
-                forward_x(s - 1)
-        if t == 0:
-            for i in range(min(C // 2, PIECES), PIECES):
-                forward_x(i)
-        for u in range(2):
-            v = part(t, p, u)
+                    if s < hops(u, d):
+                        wait_recv(rs.at[k, u, d, s], qr.at[k, u, d, s - 1])
+                        send_part(k, u, d, s)
+            if (k, s) in pass_on:
+                forward_x(pass_on[k, s])
+        if k + 1 < len(phases):
+            begin(k + 1)
+        for u in range(2):
+            came = [rs.at[k, u, d, hops(u, d)] for d in range(2)]
             for d in range(2):
-                n = hops(u, d)
-                buf = rs.at[t, u, d, n]
-                wait_recv(buf, qr.at[t, u, d, n - 1])
-                v = v + buf[...].astype(f32)
-            g[p, t, u * hb : (u + 1) * hb, :] = v.astype(bf16)
-        if t == 0:
-            finish_x()
+                wait_recv(came[d], qr.at[k, u, d, hops(u, d) - 1])
+            add_part(k, p, u, came, g.at[p, t * HF + f, u * hb : (u + 1) * hb, :])
+
+    def dots(left, right):
+        if ww % 128 == 0:
+            left, right = [jnp.concatenate(left, axis=1)], [jnp.concatenate(right, axis=0)]
+        v = None
+        for a, b in zip(left, right):
+            m = jnp.dot(a, b, preferred_element_type=f32)
+            v = m if v is None else v + m
+        return v
 
     def add_y(q, u, h, first=False):
         rr = pl.ds(u * hb + h * nr, nr)
-        v = None
-        for t in range(T):
-            m = jnp.dot(
-                g[q, t, rr, :], xc[rows(start_of(t) + q * w, w), :], preferred_element_type=f32
-            )
-            v = m if v is None else v + m
+        tf = [(t, f) for t in range(T) for f in range(HF)]
+        v = dots([g[q, t * HF + f, rr, :] for t, f in tf], [xc[at(t, f, q), :] for t, f in tf])
         if first:
             y[rr, :] = v
         else:
@@ -178,14 +215,51 @@
         for j in range(1, T):
             wait_recv(zref(lax.rem(mate[0] + R - 2 * j, R), u, h), qz.at[h, u, T + j])
 
+    tile = min(B, 256)
+
+    def add_out(t, e, h, first=False, final=False):
+        terms = {}
+        for u in range(2):
+            for k0 in range(u * hb + h * nr, u * hb + (h + 1) * nr, ww):
+                f, o = k0 // (B // HF), k0 % (B // HF)
+                terms.setdefault(e * half + o // ww, []).append((f, e * B + k0))
+
+        @pl.loop(0, B // tile)
+        def _(i):
+            rr = rows(i * tile, tile)
+            v = None
+            for q, fs in terms.items():
+                m = dots(
+                    [g[q, t * HF + f, rr, :] for f, _ in fs],
+                    [zc[rows(start_of(t) + k0, ww), :] for _, k0 in fs],
+                )
+                v = m if v is None else v + m
+            if not first:
+                v = v + o_ref[rr, :]
+            if final:
+                v = coef_a * x_ref[rr, :].astype(f32) + coef_b * y[rr, :] + coef_c * v
+                v = scale * v
+            o_ref[rr, :] = v
+
+    def mate_z(h):
+        for u in range(2):
+            wait_recv(zref(mate[0], u, h), qz.at[h, u, 0])
+
+    def far_out(h, final=False):
+        for u in range(2):
+            finish_z(h, u)
+        for t in range(1, T):
+            for e in range(2):
+                add_out(t, e, h, final=final and t == T - 1 and e == 1)
+
     for u in range(2):
         for d in range(2):
             send_g(0, u, d, 0)
+    last = half - 1
     for h in range(SLICES):
         for u in range(2):
             add_y(p, u, h, first=True)
-        last = C // 2 - 1
-        for s in range(last + 1):
+        for s in range(half):
             if s == last and h > 0:
                 for u in range(2):
                     forward_z(h - 1, u)
@@ -209,53 +283,20 @@
                 send(mine, mine, sz.at[h, u, j], qz.at[h, u, j], peer(j))
             send(mine, mine, sz.at[h, u, 0], qz.at[h, u, 0], mate)
 
-    tile = min(B, 256)
-
-    def add_out(terms, final=False):
-        @pl.loop(0, B // tile)
-        def _(i):
-            rr = rows(i * tile, tile)
-            v = jnp.zeros((tile, W), f32)
-            for t, e, u, h in terms:
-                k = e * B + u * hb + h * nr
-                for k0 in range(k, k + nr, min(w, nr)):
-                    n = min(w, nr)
-                    q, off = k0 // w, k0 % w
-                    v = v + jnp.dot(
-                        g[q, t, rr, off : off + n],
-                        zc[rows(start_of(t) + k0, n), :],
-                        preferred_element_type=f32,
-                    )
-            if final:
-                o_ref[rr, :] = scale * (y[rr, :] + coef_c * v)
-            else:
-                y[rr, :] += coef_c * v
-
-    @pl.loop(0, B // tile)
-    def _(i):
-        rr = rows(i * tile, tile)
-        y[rr, :] = coef_a * x_ref[rr, :].astype(f32) + coef_b * y[rr, :]
-
     L = SLICES - 1
-    for h in range(SLICES):
-        for u in range(2):
-            wait_recv(zref(mate[0], u, h), qz.at[h, u, 0])
     for h in range(L):
-        for u in range(2):
-            finish_z(h, u)
-    for h in range(SLICES):
-        add_out([(0, e, u, h) for e in range(2) for u in range(2)])
+        mate_z(h)
+        for e in range(2):
+            add_out(0, e, h, first=h == 0 and e == 0)
+    far_out(0)
     forward_z(L, 0)
-    for h in range(L):
-        for t in range(1, T):
-            add_out([(t, e, u, h) for e in range(2) for u in range(2)])
+    for h in range(1, L):
+        far_out(h)
     forward_z(L, 1)
-    finish_z(L, 0)
-    for t in range(1, T):
-        add_out([(t, e, 0, L) for e in range(2)])
-    finish_z(L, 1)
-    for t in range(1, T):
-        add_out([(t, e, 1, L) for e in range(2)], final=t == T - 1)
+    mate_z(L)
+    for e in range(2):
+        add_out(0, e, L)
+    far_out(L, final=True)
 
     for cp in sent:
         cp.wait_send()
@@ -267,10 +308,10 @@
     def step(x):
         B, W = x.shape
         T = R // 2
-        w = 2 * B // C
+        HF, ww = split(B, C)
         dma = pltpu.SemaphoreType.DMA
         bf16 = jnp.bfloat16
-        rs_sems = (T, 2, 2, C // 2)
+        rs_sems = (T * HF, 2, 2, C // 2)
         ag_sems = (SLICES, 2, 2, C // 2)
         return pl.pallas_call(
             functools.partial(kernel, R, C, math.sqrt(W * C)),
@@ -280,8 +321,8 @@
             scratch_shapes=[
                 pltpu.VMEM((R * B, W), bf16),
                 pltpu.VMEM((R * B, W), bf16),
-                pltpu.VMEM((T, 2, 2, C // 2 + 1, B // 2, w), bf16),
-                pltpu.VMEM((C, T, B, w), bf16),
+                pltpu.VMEM((T * HF, 2, 2, C // 2 + 1, B // 2, ww), bf16),
+                pltpu.VMEM((C, T * HF, B, ww), bf16),
                 pltpu.VMEM((B, W), jnp.float32),
                 dma((2 * T, PIECES)), dma((2 * T, PIECES)),
                 dma(rs_sems), dma(rs_sems),

time: 215 us -> 216 us (level)
  no operation moved by 1% of the time
where the time goes in v2:
time: 216 us
  Pallas kernels  211 us (98%)
  local copies, waits for them, and re-layouts  4.79 us (2%)
    pallas_call x1, Pallas kernels, step(): pl.pallas_call(functools.partial(kernel, R, C, math.sqrt(W * C)), out_sha...  211 us
    unnamed x1, local copies, waits for them, and re-layouts  4.79 us

profile of v2, /device:TPU:0, one launch (start us, length us, event | category | flops | bytes accessed | tf_op | source)
XLA Modules:
  0.0 215.8 jit_solution(16861344784446660861)
XLA Ops:
  0.0 211.0 %shard_map.17 = f32[1024,1024]{1,0:T(8,128)} custom-call(bf16[1024,1024]{1,0:T(8,128)(2,1)} %x_ref.1), custom_call_target="tpu_custom_call" | custom-call | tf_op jit(solution)/shard_map/pallas_call | solution.py:316
  211.0 4.8 %copy.3 = f32[1024,1024]{1,0:T(8,128)} copy(f32[1024,1024]{1,0:T(8,128)} %shard_map.17) | data formatting | bytes 8388608
